TPU v7x, 256 devices: a whole 4x4x8 slice. The times are simulated.
256 devices in a mesh: leaf: 32 (over z, x), rank: 4 (over y), rhs: 2 (over core).
Axes of the slice: x: 4, y: 4, z: 8, core: 2. Of those that a mesh axis runs over, the one named last changes fastest.
Arguments:
- rhs: float32 [65536, 512], P(('leaf', 'rank'), 'rhs'), parts along dimension 1, may hold values from -40 to 40
- order: int32 [65536], P(('leaf', 'rank')), may hold values from 0 to 65535, as said below
- diag: float32 [65536], P(('leaf', 'rank')), may hold values from 2 to 8
- blocks: bfloat16 [1536, 128, 128], P(('leaf', 'rank')), may hold values from -0.3125 to 0.3125
- near_rows: int32 [1536], P(('leaf', 'rank')), may hold values from 0 to 511, as said below
- near_cols: int32 [1536], P(('leaf', 'rank')), may hold values from 0 to 511, as said below
- gen_u: bfloat16 [5, 65536, 128], P(None, 'leaf', 'rank'), may hold values from -0.5 to 0.5
- gen_v: bfloat16 [5, 65536, 128], P(None, 'leaf', 'rank'), may hold values from -0.03125 to 0.03125
Outputs:
- solution: float32 [65536, 512], P(('leaf', 'rank'), 'rhs'), parts along dimension 1
- residual: float32 [65536, 512], P(('leaf', 'rank'), 'rhs'), parts along dimension 1
There are 2 independent parts, one for each index of `rhs`. A program takes and returns all parts, laid end to end along the dimension named above; an argument that names none is the same for every part. Nothing has to cross between parts.
Inputs may be any that keep to these rules, and one draw needn't show every extreme that they name: `order`: each aligned run of 512 entries is a permutation of the panel numbers of that run. `near_rows`: block k's row is one of the 4 block rows of the device that holds block k; every block row is named, at least once by a block whose column equals it. `near_cols`: block k's column lies in the same subtree of 2048 panels as its row, at most 4 block columns away from it.
All inputs are finite; a program needn't handle non-finite values.
Results may differ from a plain program's by a relative error of at most 0.0035.
Values may be sent and summed in bfloat16 or wider, within the bound.
A program may use at most 64 MiB of HBM per device.

v0:
```python
import jax
import jax.numpy as jnp
from jax import lax
from jax.sharding import PartitionSpec as P

EPSILON = 1e-06


def from_partner(value, axis, apart):
    mask = 2**apart
    pairs = [(source, source ^ mask) for source in range(lax.axis_size(axis))]
    return lax.ppermute(value, axis, pairs)


def local(rhs, order, diag, blocks, near_rows, near_cols, gen_u, gen_v):
    panel_count, columns_count = rhs.shape
    levels = gen_v.shape[0]
    leaf_panels = gen_v.shape[1]
    block_size = blocks.shape[1]
    rows_dev = panel_count // block_size
    rows_leaf = leaf_panels // block_size
    device = lax.axis_index(("leaf", "rank"))
    leaf_id = lax.axis_index("leaf")
    local_order = order - device * panel_count
    local_rows = near_rows - device * rows_dev
    local_cols = near_cols - leaf_id * rows_leaf
    selector = (jnp.arange(rows_dev, dtype=jnp.int32)[:, None] == local_rows[None, :]).astype(
        jnp.float32
    )

    def tree_sums(coeffs):
        partial_value = [coeffs[level] for level in range(levels)]
        sibling = []
        for level in range(levels):
            stacked = jnp.stack(partial_value[level:], 0)
            received = from_partner(stacked, "leaf", level)
            sibling.append(received[0])
            for upper in range(level + 1, levels):
                partial_value[upper] = partial_value[upper] + received[upper - level]
        return jnp.stack(sibling, 0)

    def apply(vector):
        narrow = vector.astype(jnp.bfloat16)
        subtree = lax.all_gather(narrow, "rank", axis=0, tiled=True)
        coeffs = jnp.einsum("lpk,pn->lkn", gen_v, subtree, preferred_element_type=jnp.float32)
        column_blocks = subtree.reshape(rows_leaf, block_size, columns_count)[local_cols]
        sibling = tree_sums(coeffs).astype(jnp.bfloat16)
        products = jnp.einsum(
            "kij,kjn->kin", blocks, column_blocks, preferred_element_type=jnp.float32
        )
        near = jnp.einsum(
            "rk,kin->rin", selector, products, precision=lax.Precision.HIGHEST
        ).reshape(panel_count, columns_count)
        far = lax.psum_scatter(
            jnp.einsum("lpk,lkn->pn", gen_u, sibling, preferred_element_type=jnp.float32),
            "rank",
            scatter_dimension=0,
            tiled=True,
        )
        return diag[:, None] * vector + near + far

    start = rhs[local_order]
    beta = jnp.sqrt(lax.psum(jnp.sum(start * start, axis=0), ("leaf", "rank")) + EPSILON)
    basis_one = start / beta
    image_one = apply(basis_one)
    h11 = lax.psum(jnp.sum(basis_one * image_one, axis=0), ("leaf", "rank"))
    rest_one = image_one - h11 * basis_one
    h21 = jnp.sqrt(lax.psum(jnp.sum(rest_one * rest_one, axis=0), ("leaf", "rank")) + EPSILON)
    basis_two = rest_one / h21
    image_two = apply(basis_two)
    h12, h22 = lax.psum(
        (jnp.sum(basis_one * image_two, axis=0), jnp.sum(basis_two * image_two, axis=0)),
        ("leaf", "rank"),
    )
    rest_two = image_two - h12 * basis_one - h22 * basis_two
    h32 = jnp.sqrt(lax.psum(jnp.sum(rest_two * rest_two, axis=0), ("leaf", "rank")) + EPSILON)
    r_one = jnp.sqrt(h11 * h11 + h21 * h21)
    cos_one = h11 / r_one
    sin_one = h21 / r_one
    top = cos_one * h12 + sin_one * h22
    low = cos_one * h22 - sin_one * h12
    r_two = jnp.sqrt(low * low + h32 * h32)
    y_two = low / r_two * (-sin_one * beta) / r_two
    y_one = (cos_one * beta - top * y_two) / r_one
    tree_solution = y_one * basis_one + y_two * basis_two
    tree_residual = (
        (beta - y_one * h11 - y_two * h12) * basis_one
        - (y_one * h21 + y_two * h22) * basis_two
        - y_two * rest_two
    )
    solution = jnp.zeros_like(rhs).at[local_order].set(tree_solution)
    residual = jnp.zeros_like(rhs).at[local_order].set(tree_residual)
    return (solution, residual)


def solution(mesh):
    in_specs = (
        P(("leaf", "rank"), "rhs"),
        P(("leaf", "rank")),
        P(("leaf", "rank")),
        P(("leaf", "rank"), None, None),
        P(("leaf", "rank")),
        P(("leaf", "rank")),
        P(None, "leaf", "rank"),
        P(None, "leaf", "rank"),
    )
    out_specs = (P(("leaf", "rank"), "rhs"), P(("leaf", "rank"), "rhs"))
    return jax.shard_map(local, mesh=mesh, in_specs=in_specs, out_specs=out_specs, check_vma=False)
```

profile of v0, /device:TPU:8, one launch (start us, length us, event | category | flops | bytes accessed | tf_op | source)
XLA Modules:
  0.0 1938.2 jit_solution(10514694611025003767)
XLA Ops:
  8.0 2.7 gather_fusion
  10.8 346.4 %psum.42 = f32[256]{0:T(256)S(1)} all-reduce(f32[256]{0:T(256)S(1)} %multiply_reduce_fusion.5), channel_id=1, replica_groups=mesh['leaf'=32,'rank'=4,'rhs'=2] {'leaf','rank'}, use_global_device_ids=true, to_apply=%region_1.0 | all-reduce | flops 256 | bytes 2048 | tf_op jit(solution)/shard_map/psum | solution.py:63
  357.9 23.9 %all-gather.3.cloned.1.call-done = bf16[2048,256]{1,0:T(8,128)(2,1)} async-done(((bf16[512,256]{1,0:T(8,128)(2,1)}), bf16[2048,256]{1,0:T(8,128)(2,1)}) %all-gather.3.cloned.1.call-update) | async-done | bytes 1048592 | tf_op jit(solution)/shard_map/all_gather | solution.py:44
  385.0 3.9 collective-permute-done
  388.9 3.1 collective-permute-start.1
  391.9 3.5 collective-permute-done.1
  397.1 3.8 collective-permute-done.2
  402.8 3.3 collective-permute-done.3
  406.2 6.2 collective-permute-start.4
  421.8 27.5 %reduce-scatter.3.cloned.1.call-done = f32[512,256]{1,0:T(8,128)} async-done(((f32[2048,256]{1,0:T(8,128)}), f32[512,256]{1,0:T(8,128)}) %reduce-scatter.3.cloned.1.call-update) | async-done | bytes 524304 | tf_op jit(solution)/shard_map/reduce_scatter | solution.py:54
  450.5 344.0 %psum.43 = f32[256]{0:T(256)S(1)} all-reduce(f32[256]{0:T(256)S(1)} %multiply_reduce_fusion.4), channel_id=1, replica_groups=mesh['leaf'=32,'rank'=4,'rhs'=2] {'leaf','rank'}, use_global_device_ids=true, to_apply=%region_4.0 | all-reduce | flops 256 | bytes 2048 | tf_op jit(solution)/shard_map/psum | solution.py:66
  795.7 347.8 %psum.44 = f32[256]{0:T(256)S(1)} all-reduce(f32[256]{0:T(256)S(1)} %get-tuple-element.10), channel_id=1, replica_groups=mesh['leaf'=32,'rank'=4,'rhs'=2] {'leaf','rank'}, use_global_device_ids=true, to_apply=%region_6.0 | all-reduce | flops 256 | bytes 2048 | tf_op jit(solution)/shard_map/psum | solution.py:68
  1144.4 20.1 %all-gather.5.cloned.1.call-done = bf16[2048,256]{1,0:T(8,128)(2,1)} async-done(((bf16[512,256]{1,0:T(8,128)(2,1)}), bf16[2048,256]{1,0:T(8,128)(2,1)}) %all-gather.5.cloned.1.call-update) | async-done | bytes 1048592 | tf_op jit(solution)/shard_map/all_gather | solution.py:44
  1167.6 3.9 collective-permute-done.5
  1171.5 3.1 collective-permute-start.6
  1174.6 3.5 collective-permute-done.6
  1179.7 3.8 collective-permute-done.7
  1185.4 3.3 collective-permute-done.8
  1188.8 6.4 collective-permute-start.9
  1206.5 25.5 %reduce-scatter.5.cloned.1.call-done = f32[512,256]{1,0:T(8,128)} async-done(((f32[2048,256]{1,0:T(8,128)}), f32[512,256]{1,0:T(8,128)}) %reduce-scatter.5.cloned.1.call-update) | async-done | bytes 524304 | tf_op jit(solution)/shard_map/reduce_scatter | solution.py:54
  1233.3 344.0 %all-reduce = (f32[256]{0:T(256)S(1)}, f32[256]{0:T(256)S(1)}) all-reduce(f32[256]{0:T(256)S(1)} %get-tuple-element.3, f32[256]{0:T(256)S(1)} %get-tuple-element.2), channel_id=1, replica_groups=mesh['leaf'=32,'rank'=4,'rhs'=2] {'leaf','rank'}, use_global_device_ids=true, to_apply=%region_11.0 | all-reduce | flops 512 | bytes 4096 | tf_op jit(solution)/shard_map/psum | solution.py:71
  1577.5 347.8 %psum.47 = f32[256]{0:T(256)S(1)} all-reduce(f32[256]{0:T(256)S(1)} %multiply_reduce_fusion), channel_id=1, replica_groups=mesh['leaf'=32,'rank'=4,'rhs'=2] {'leaf','rank'}, use_global_device_ids=true, to_apply=%region_13.0 | all-reduce | flops 256 | bytes 2048 | tf_op jit(solution)/shard_map/psum | solution.py:76
  1925.3 3.1 scatter_custom_fusion
  1928.4 3.2 scatter_custom_fusion.1
  (86 shorter events, 40.5 us)
Async XLA Ops:
  7.2 407.0 %copy-start = (bf16[5,2048,32]{1,2,0:T(8,128)(2,1)S(1)}, bf16[5,2048,32]{1,2,0:T(8,128)(2,1)}, u32[]{:S(2)}) copy-start(bf16[5,2048,32]{1,2,0:T(8,128)(2,1)} %param.14) | copy-start | bytes 1966084
  7.2 374.7 %all-gather.3.cloned.1.call-start = ((), (), s32[]{:S(2)}) async-start(), calls=%async_computation.2 | async-start | bytes 1310720 | tf_op jit(solution)/shard_map/all_gather | solution.py:44
  8.0 373.9 %copy-start.3 = (bf16[5,2048,32]{1,2,0:T(8,128)(2,1)S(1)}, bf16[5,2048,32]{1,2,0:T(8,128)(2,1)}, u32[]{:S(2)}) copy-start(bf16[5,2048,32]{1,2,0:T(8,128)(2,1)} %param.15) | copy-start | bytes 1966084
  357.9 91.4 %reduce-scatter.3.cloned.1.call-start = ((), (), s32[]{:S(2)}) async-start(), calls=%async_computation.3 | async-start | bytes 2621440 | tf_op jit(solution)/shard_map/reduce_scatter | solution.py:54
  383.4 5.4 collective-permute-start
  388.9 6.6 collective-permute-start.1
  395.5 5.4 collective-permute-start.2
  400.9 5.3 collective-permute-start.3
  406.2 8.0 collective-permute-start.4
  414.1 2.0 copy-start.7
  414.1 2.0 copy-start.8
  414.2 2.0 copy-start.1
  416.1 1.0 copy-start.5
  416.1 748.4 %all-gather.5.cloned.1.call-start = ((), (), s32[]{:S(2)}) async-start(), calls=%async_computation.4 | async-start | bytes 1310720 | tf_op jit(solution)/shard_map/all_gather | solution.py:44
  420.8 28.5 %copy-start.6 = (f32[512]{0:T(512)S(1)}, f32[512]{0:T(512)}, u32[]{:S(2)}) copy-start(f32[512]{0:T(512)} %param.10) | copy-start | bytes 6148
  421.8 742.7 %copy-start.4 = (bf16[5,2048,32]{1,2,0:T(8,128)(2,1)S(1)}, bf16[5,2048,32]{1,2,0:T(8,128)(2,1)}, u32[]{:S(2)}) copy-start(bf16[5,2048,32]{1,2,0:T(8,128)(2,1)} %param.15) | copy-start | bytes 1966084
  1144.3 87.8 %reduce-scatter.5.cloned.1.call-start = ((), (), s32[]{:S(2)}) async-start(), calls=%async_computation.5 | async-start | bytes 2621440 | tf_op jit(solution)/shard_map/reduce_scatter | solution.py:54
  1166.0 5.4 collective-permute-start.5
  1171.5 6.6 collective-permute-start.6
  1178.1 5.4 collective-permute-start.7
  1183.5 5.3 collective-permute-start.8
  1188.8 8.1 collective-permute-start.9
  1196.9 1.9 copy-start.2
Sparse Core Ops, SparseCore 0:
  358.0 23.7 all-gather.2
  416.2 33.0 reduce-scatter.2
  1144.4 20.0 all-gather.4
  1199.0 33.0 reduce-scatter.4
where the time goes:
time: 1940 us
  blocking collectives  1730 us (89%)
  waiting for transfers between devices  129 us (7%)
  starting transfers between devices  29.2 us (2%)
    psum x1, blocking collectives, local(): lax.psum(jnp.sum(rest_one * rest_one, axis=0), ('leaf', 'rank')) + EPSILON  348 us
    psum x1, blocking collectives, local(): lax.psum(jnp.sum(rest_two * rest_two, axis=0), ('leaf', 'rank')) + EPSILON  348 us
    psum x1, blocking collectives, local(): lax.psum(jnp.sum(start * start, axis=0), ('leaf', 'rank')) + EPSILON  346 us
    psum x1, blocking collectives, local(): lax.psum((jnp.sum(basis_one * image_two, axis=0), jnp.sum(basis_two * ima...  344 us
    psum x1, blocking collectives, local(): h11 = lax.psum(jnp.sum(basis_one * image_one, axis=0), ('leaf', 'rank'))  344 us
    reduce_scatter x2, waiting for transfers between devices, apply(): lax.psum_scatter(jnp.einsum('lpk,lkn->pn', gen_u, sibling, preferred_elem...  53 us
    all_gather x2, waiting for transfers between devices, apply(): subtree = lax.all_gather(narrow, 'rank', axis=0, tiled=True)  44 us
  transfers between devices with their start and end apart: 14, of which 14 were waited for; matrix products, arithmetic and copies ran while one was open for 1% of the time, Pallas kernels for 0%

commit v1 on v0

--- a/solution.py
+++ b/solution.py
@@ -69,8 +69,10 @@
     basis_two = rest_one / h21
     image_two = apply(basis_two)
     h12, h22 = lax.psum(
-        (jnp.sum(basis_one * image_two, axis=0), jnp.sum(basis_two * image_two, axis=0)),
-        ("leaf", "rank"),
+        lax.psum(
+            (jnp.sum(basis_one * image_two, axis=0), jnp.sum(basis_two * image_two, axis=0)), "rank"
+        ),
+        "leaf",
     )
     rest_two = image_two - h12 * basis_one - h22 * basis_two
     h32 = jnp.sqrt(lax.psum(jnp.sum(rest_two * rest_two, axis=0), ("leaf", "rank")) + EPSILON)

time: 1940 us -> 1670 us (0.86)
  blocking collectives: 1730 us -> 1470 us
    psum x1, blocking collectives: 344 us -> 9.53 us  [local(): lax.psum((jnp.sum(basis_one * image_two, axis=0), jnp.sum(basis_two * ima...]
    psum x0 -> x1, blocking collectives: none -> 75 us  [local(): lax.psum(lax.psum((jnp.sum(basis_one * image_two, axis=0), jnp.sum(basis_...]
where the time goes in v1:
time: 1670 us
  blocking collectives  1470 us (88%)
  waiting for transfers between devices  129 us (8%)
  starting transfers between devices  29.2 us (2%)
    psum x1, blocking collectives, local(): lax.psum(jnp.sum(rest_one * rest_one, axis=0), ('leaf', 'rank')) + EPSILON  348 us
    psum x1, blocking collectives, local(): lax.psum(jnp.sum(start * start, axis=0), ('leaf', 'rank')) + EPSILON  346 us
    psum x1, blocking collectives, local(): h11 = lax.psum(jnp.sum(basis_one * image_one, axis=0), ('leaf', 'rank'))  344 us
    psum x1, blocking collectives, local(): lax.psum(jnp.sum(rest_two * rest_two, axis=0), ('leaf', 'rank')) + EPSILON  343 us
    psum x1, blocking collectives, local(): lax.psum(lax.psum((jnp.sum(basis_one * image_two, axis=0), jnp.sum(basis_...  75 us
    reduce_scatter x2, waiting for transfers between devices, apply(): lax.psum_scatter(jnp.einsum('lpk,lkn->pn', gen_u, sibling, preferred_elem...  53 us
    all_gather x2, waiting for transfers between devices, apply(): subtree = lax.all_gather(narrow, 'rank', axis=0, tiled=True)  44 us
  transfers between devices with their start and end apart: 14, of which 14 were waited for; matrix products, arithmetic and copies ran while one was open for 1% of the time, Pallas kernels for 0%

profile of v1, /device:TPU:8, one launch (start us, length us, event | category | flops | bytes accessed | tf_op | source)
XLA Modules:
  0.0 1674.0 jit_solution(6604439461903654605)
XLA Ops:
  10.8 346.4 %psum.56 = f32[256]{0:T(256)S(1)} all-reduce(f32[256]{0:T(256)S(1)} %multiply_reduce_fusion.5), channel_id=1, replica_groups=mesh['leaf'=32,'rank'=4,'rhs'=2] {'leaf','rank'}, use_global_device_ids=true, to_apply=%region_1.0 | all-reduce | flops 256 | bytes 2048 | tf_op jit(solution)/shard_map/psum | solution.py:63
  357.9 23.9 %all-gather.3.cloned.1.call-done = bf16[2048,256]{1,0:T(8,128)(2,1)} async-done(((bf16[512,256]{1,0:T(8,128)(2,1)}), bf16[2048,256]{1,0:T(8,128)(2,1)}) %all-gather.3.cloned.1.call-update) | async-done | bytes 1048592 | tf_op jit(solution)/shard_map/all_gather | solution.py:44
  385.0 3.9 collective-permute-done
  388.9 3.1 collective-permute-start.1
  391.9 3.5 collective-permute-done.1
  397.1 3.8 collective-permute-done.2
  402.8 3.3 collective-permute-done.3
  406.2 6.2 collective-permute-start.4
  421.8 27.5 %reduce-scatter.3.cloned.1.call-done = f32[512,256]{1,0:T(8,128)} async-done(((f32[2048,256]{1,0:T(8,128)}), f32[512,256]{1,0:T(8,128)}) %reduce-scatter.3.cloned.1.call-update) | async-done | bytes 524304 | tf_op jit(solution)/shard_map/reduce_scatter | solution.py:54
  450.5 344.0 %psum.57 = f32[256]{0:T(256)S(1)} all-reduce(f32[256]{0:T(256)S(1)} %multiply_reduce_fusion.4), channel_id=1, replica_groups=mesh['leaf'=32,'rank'=4,'rhs'=2] {'leaf','rank'}, use_global_device_ids=true, to_apply=%region_4.0 | all-reduce | flops 256 | bytes 2048 | tf_op jit(solution)/shard_map/psum | solution.py:66
  795.7 347.8 %psum.58 = f32[256]{0:T(256)S(1)} all-reduce(f32[256]{0:T(256)S(1)} %get-tuple-element.12), channel_id=1, replica_groups=mesh['leaf'=32,'rank'=4,'rhs'=2] {'leaf','rank'}, use_global_device_ids=true, to_apply=%region_6.0 | all-reduce | flops 256 | bytes 2048 | tf_op jit(solution)/shard_map/psum | solution.py:68
  1144.4 20.1 %all-gather.5.cloned.1.call-done = bf16[2048,256]{1,0:T(8,128)(2,1)} async-done(((bf16[512,256]{1,0:T(8,128)(2,1)}), bf16[2048,256]{1,0:T(8,128)(2,1)}) %all-gather.5.cloned.1.call-update) | async-done | bytes 1048592 | tf_op jit(solution)/shard_map/all_gather | solution.py:44
  1167.6 3.8 collective-permute-done.5
  1171.5 3.1 collective-permute-start.6
  1174.6 3.5 collective-permute-done.6
  1179.7 3.8 collective-permute-done.7
  1185.5 3.3 collective-permute-done.8
  1188.8 6.4 collective-permute-start.9
  1206.5 25.6 %reduce-scatter.5.cloned.1.call-done = f32[512,256]{1,0:T(8,128)} async-done(((f32[2048,256]{1,0:T(8,128)}), f32[512,256]{1,0:T(8,128)}) %reduce-scatter.5.cloned.1.call-update) | async-done | bytes 524304 | tf_op jit(solution)/shard_map/reduce_scatter | solution.py:54
  1233.3 9.5 all-reduce.1
  1242.9 75.0 %all-reduce = (f32[256]{0:T(256)S(1)}, f32[256]{0:T(256)S(1)}) all-reduce(f32[256]{0:T(256)S(1)} %get-tuple-element.6, f32[256]{0:T(256)S(1)} %get-tuple-element.7), channel_id=1, replica_groups=mesh['leaf'=32,'rank'=4,'rhs'=2] {'leaf'}, use_global_device_ids=true, to_apply=%region_13.0 | all-reduce | flops 512 | bytes 4096 | tf_op jit(solution)/shard_map/psum | solution.py:71
  1318.1 343.0 %psum.63 = f32[256]{0:T(256)S(1)} all-reduce(f32[256]{0:T(256)S(1)} %multiply_reduce_fusion), channel_id=1, replica_groups=mesh['leaf'=32,'rank'=4,'rhs'=2] {'leaf','rank'}, use_global_device_ids=true, to_apply=%region_15.0 | all-reduce | flops 256 | bytes 2048 | tf_op jit(solution)/shard_map/psum | solution.py:78
  1661.1 3.1 scatter_custom_fusion
  1664.2 3.2 scatter_custom_fusion.1
  (87 shorter events, 43.2 us)
Async XLA Ops:
  7.2 407.0 %copy-start = (bf16[5,2048,32]{1,2,0:T(8,128)(2,1)S(1)}, bf16[5,2048,32]{1,2,0:T(8,128)(2,1)}, u32[]{:S(2)}) copy-start(bf16[5,2048,32]{1,2,0:T(8,128)(2,1)} %param.14) | copy-start | bytes 1966084
  7.2 374.7 %all-gather.3.cloned.1.call-start = ((), (), s32[]{:S(2)}) async-start(), calls=%async_computation.2 | async-start | bytes 1310720 | tf_op jit(solution)/shard_map/all_gather | solution.py:44
  8.0 373.9 %copy-start.3 = (bf16[5,2048,32]{1,2,0:T(8,128)(2,1)S(1)}, bf16[5,2048,32]{1,2,0:T(8,128)(2,1)}, u32[]{:S(2)}) copy-start(bf16[5,2048,32]{1,2,0:T(8,128)(2,1)} %param.15) | copy-start | bytes 1966084
  357.9 91.4 %reduce-scatter.3.cloned.1.call-start = ((), (), s32[]{:S(2)}) async-start(), calls=%async_computation.3 | async-start | bytes 2621440 | tf_op jit(solution)/shard_map/reduce_scatter | solution.py:54
  383.4 5.4 collective-permute-start
  388.9 6.6 collective-permute-start.1
  395.5 5.4 collective-permute-start.2
  400.9 5.3 collective-permute-start.3
  406.2 8.0 collective-permute-start.4
  414.1 2.0 copy-start.7
  414.1 2.0 copy-start.8
  414.2 2.1 copy-start.1
  416.1 1.0 copy-start.5
  416.1 748.4 %all-gather.5.cloned.1.call-start = ((), (), s32[]{:S(2)}) async-start(), calls=%async_computation.4 | async-start | bytes 1310720 | tf_op jit(solution)/shard_map/all_gather | solution.py:44
  420.8 28.4 %copy-start.6 = (f32[512]{0:T(512)S(1)}, f32[512]{0:T(512)}, u32[]{:S(2)}) copy-start(f32[512]{0:T(512)} %param.10) | copy-start | bytes 6148
  421.8 742.7 %copy-start.4 = (bf16[5,2048,32]{1,2,0:T(8,128)(2,1)S(1)}, bf16[5,2048,32]{1,2,0:T(8,128)(2,1)}, u32[]{:S(2)}) copy-start(bf16[5,2048,32]{1,2,0:T(8,128)(2,1)} %param.15) | copy-start | bytes 1966084
  1144.3 87.8 %reduce-scatter.5.cloned.1.call-start = ((), (), s32[]{:S(2)}) async-start(), calls=%async_computation.5 | async-start | bytes 2621440 | tf_op jit(solution)/shard_map/reduce_scatter | solution.py:54
  1166.0 5.4 collective-permute-start.5
  1171.5 6.6 collective-permute-start.6
  1178.1 5.4 collective-permute-start.7
  1183.5 5.3 collective-permute-start.8
  1188.8 8.1 collective-permute-start.9
  1196.9 1.9 copy-start.2
Sparse Core Ops, SparseCore 0:
  358.0 23.7 all-gather.2
  416.2 33.0 reduce-scatter.2
  1144.4 20.0 all-gather.4
  1199.0 33.0 reduce-scatter.4
